TPU v7x, 256 devices: a whole 4x4x8 slice. The times are simulated.
256 devices in a mesh: row: 16 (over z_hi, y), col: 16 (over z_lo, x, core).
Axes of the slice: x: 4, y: 4, z: 8 (z_hi: 4, z_lo: 2; z = z_hi * 2 + z_lo), core: 2. Of those that a mesh axis runs over, the one named last changes fastest.
Arguments:
- a11: float32 [256, 256], replicated, as said below
- linv11: float32 [256, 256], replicated, as said below
- a21: float32 [16384, 256], P(('row', 'col')), may hold values from -6 to 6
- l21: float32 [16384, 256], P(('row', 'col')), may hold values from -0.4 to 0.4
- a22: float32 [16384, 16384], P('row', 'col'), may hold values from -6 to 6
Outputs:
- diag_block: float32 [256, 256], replicated
- panel: float32 [16384, 256], P(('row', 'col'))
- trailing: float32 [16384, 16384], P('row', 'col')
Inputs may be any that keep to these rules, and one draw needn't show every extreme that they name: `a11`: symmetric. `linv11`: lower triangular with a positive diagonal.
All inputs are finite; a program needn't handle non-finite values.
Results may differ from a plain program's by a relative error of at most 0.00005.
Values sent between devices are 32-bit elements; how exact they have to be, the bound alone decides.
A program may use at most 64 MiB of HBM per device.

v0:
```python
import jax
import jax.numpy as jnp
from jax import lax
from jax.sharding import PartitionSpec as P


def spread(value, axis, source):
    kept = jnp.where(lax.axis_index(axis) == source, value, 0).astype(value.dtype)
    return lax.psum(kept, axis)


def mult(a, b):
    return jnp.dot(a, b, precision=lax.Precision.HIGHEST, preferred_element_type=jnp.float32)


def body(a11, linv11, a21, l21, a22):
    width = a21.shape[1]
    diag_block = mult(mult(linv11, a11), linv11.T)
    correction = 0.5 * mult(l21, diag_block)
    half = mult(a21, linv11.T) - correction
    panel = half - correction
    packed = jnp.concatenate([half, l21], axis=1)
    n_row = lax.axis_size("row")
    n_col = lax.axis_size("col")
    groups = n_row // n_col
    mine = lax.all_gather(packed, "col", axis=0, tiled=True)
    col_index = lax.axis_index("col")
    parts = spread(mine, "row", col_index * groups + 0)
    flipped = jnp.concatenate([parts[:, width:], parts[:, :width]], axis=1)
    trailing = a22 - mult(mine, flipped.T)
    return (diag_block, panel, trailing)


def solution(mesh):
    return jax.shard_map(
        body,
        mesh=mesh,
        in_specs=(P(), P(), P(("row", "col"), None), P(("row", "col"), None), P("row", "col")),
        out_specs=(P(), P(("row", "col"), None), P("row", "col")),
        check_vma=False,
    )
```

profile of v0, /device:TPU:6, one launch (start us, length us, event | category | flops | bytes accessed | tf_op | source)
XLA Modules:
  0.0 253.6 jit_solution(17430890461005125020)
XLA Ops:
  7.2 0.0 copy-start
  7.2 0.0 copy-start.3
  7.2 0.0 all-gather.2.cloned.1.call-start
  7.2 0.9 copy-done
  8.1 1.3 fusion.7
  9.5 0.4 fusion.8
  9.9 0.0 copy-start.2
  9.9 1.2 fusion.3
  11.1 1.8 fusion.6
  12.9 0.0 copy-done.3
  12.9 0.7 pad_maximum_fusion
  13.6 0.0 all-gather.2.cloned.1.call-update
  13.6 0.0 all-reduce.2.cloned.1.call-start
  13.7 38.5 %all-gather.2.cloned.1.call-done = f32[1024,512]{1,0:T(8,128)} async-done(((f32[64,512]{1,0:T(8,128)}), f32[1024,512]{1,0:T(8,128)}) %all-gather.2.cloned.1.call-update) | async-done | bytes 2097168 | tf_op jit(solution)/shard_map/all_gather | solution.py:26
  52.1 1.5 broadcast_select_fusion
  53.7 0.0 copy-done.2
  53.7 0.0 all-reduce.2.cloned.1.call-update
  53.7 0.0 copy-start.1
  53.7 181.5 %all-reduce.2.cloned.1.call-done = f32[1024,512]{1,0:T(8,128)} async-done(((f32[1024,512]{1,0:T(8,128)}), f32[1024,512]{1,0:T(8,128)}) %all-reduce.2.cloned.1.call-update) | async-done | bytes 2097168 | tf_op jit(solution)/shard_map/psum | solution.py:9
  235.2 1.7 fusion.5
  236.9 0.0 copy-done.1
  236.9 9.9 %convolution_subtract_fusion = f32[1024,1024]{1,0:T(8,128)} fusion(f32[1024,1024]{1,0:T(8,128)} %param.9, f32[1024,512]{1,0:T(8,128)S(1)} %copy-done.1, f32[1024,256]{1,0:T(8,128)S(1)} %get-tuple-element.4, f32[1024,256]{1,0:T(8,128)S(1)} %get-tuple-element.3), kind=kOutput, calls=%fused_computation | convolution fusion | flops 6444023808 | bytes 12582912 | tf_op jit(solution)/shard_map/dot_general | solution.py:13
Async XLA Ops:
  7.2 1.0 copy-start
  7.2 5.7 %copy-start.3 = (f32[64,256]{1,0:T(8,128)S(1)}, f32[64,256]{1,0:T(8,128)}, u32[]{:S(2)}) copy-start(f32[64,256]{1,0:T(8,128)} %param.8) | copy-start | bytes 196612
  7.2 44.9 %all-gather.2.cloned.1.call-start = ((), (), s32[]{:S(2)}) async-start(), calls=%async_computation | async-start | bytes 2228224 | tf_op jit(solution)/shard_map/all_gather | solution.py:26
  9.9 43.8 %copy-start.2 = (f32[256,256]{1,0:T(8,128)}, f32[256,256]{1,0:T(8,128)S(1)}, u32[]{:S(2)}) copy-start(f32[256,256]{1,0:T(8,128)S(1)} %fusion.8) | copy-start | bytes 786436
  13.6 221.6 %all-reduce.2.cloned.1.call-start = ((), (), s32[]{:S(2)}) async-start(), calls=%async_computation.1 | async-start | bytes 4194304 | tf_op jit(solution)/shard_map/psum | solution.py:9
  53.7 183.2 %copy-start.1 = (f32[1024,512]{1,0:T(8,128)S(1)}, f32[1024,512]{1,0:T(8,128)}, u32[]{:S(2)}) copy-start(f32[1024,512]{1,0:T(8,128)} %all-gather.2.cloned.1.call-done) | copy-start | bytes 6291460
Sparse Core Ops, SparseCore 0:
  13.7 38.3 all-gather.1
  55.3 179.8 all-reduce.1
where the time goes:
time: 255 us; the launch traced here: 254 us
  waiting for transfers between devices  220 us (86%)
  matrix products  14.6 us (6%)
  between operations  14.1 us (6%)
  local copies, waits for them, and re-layouts  2.58 us (1%)
    psum x1, waiting for transfers between devices, spread(): return lax.psum(kept, axis)  182 us
    all_gather x1, waiting for transfers between devices, body(): mine = lax.all_gather(packed, 'col', axis=0, tiled=True)  38.5 us
    dot_general x5, matrix products, mult(): jnp.dot(a, b, precision=lax.Precision.HIGHEST, preferred_element_type=jnp...  14.6 us
  transfers between devices with their start and end apart: 2, of which 2 were waited for; matrix products, arithmetic and copies ran while one was open for 0% of the time, Pallas kernels for 0%

commit v1 on v0

v1 whole, which is shorter than its diff:
```python
import jax
import jax.numpy as jnp
from jax import lax
from jax.experimental import pallas as pl
from jax.experimental.pallas import tpu as pltpu
from jax.sharding import PartitionSpec as P

F32 = jnp.float32
BF16 = jnp.bfloat16
MESH = pl.DeviceIdType.MESH
A, L = 0, 1


def split(x):
    hi = x.astype(BF16)
    return hi, (x - hi.astype(F32)).astype(BF16)


def mult(a, b):
    return jnp.dot(a, b, precision=lax.Precision.HIGHEST, preferred_element_type=F32)


def nn(a, b):
    return jnp.dot(a, b, preferred_element_type=F32)


def nt(a, b):
    return lax.dot_general(a, b, (((1,), (1,)), ((), ())), preferred_element_type=F32)


def chunk_of(col, z, y):
    zp, yp, lop, xp = col // 4, col % 4, col // 8, (col // 2) % 4
    step = (z - zp + 4) % 4
    xj = (yp + 2 + xp - y + 4) % 4
    lo = (lop + 1 - step % 2) % 2
    return lo * 8 + xj * 2 + step // 2


def cell_of(panel, chunk):
    zp, yp, lop, xp = panel // 4, panel % 4, panel // 8, (panel // 2) % 4
    lo, xj, core = chunk // 8, (chunk // 2) % 4, chunk % 2
    step = 2 * core + 1 - (lo + lop) % 2
    return ((zp + step) % 4) * 4 + (yp + 2 - xj + xp + 4) % 4


def kernel(a11, linv, a21, l21, a22, diag_o, panel_o, out, row_a, row_l, col_a, col_l,
           r_hi, r_lo, w_hi, w_lo, big, send_sem, row_sem, col_sem, in_sem, out_sem):
    r = lax.axis_index("row")
    p = lax.axis_index("col")
    z, y = r // 4, r % 4
    lo, x, k = p // 8, (p // 2) % 4, p % 2
    rows = (row_a, row_l)
    cols = (col_a, col_l)
    own = (a21, l21)

    sib = (r, lo * 8 + x * 2 + (1 - k))
    par = (r, (1 - lo) * 8 + x * 2 + k)
    xu = (r, lo * 8 + ((x + 1) % 4) * 2 + k)
    xd = (r, lo * 8 + ((x + 3) % 4) * 2 + k)
    zu = (((z + 1) % 4) * 4 + y, p)
    zd = (((z + 3) % 4) * 4 + y, p)
    yu = (z * 4 + (y + 1) % 4, p)
    yd = (z * 4 + (y + 3) % 4, p)
    t_to = (cell_of(r, p), r)
    t_from = (p, chunk_of(p, z, y))

    barrier = pltpu.get_barrier_semaphore()
    for peer in (sib, par, xu, xd, zu, zd, yu, yd, t_to, t_from):
        pl.semaphore_signal(barrier, inc=1, device_id=peer, device_id_type=MESH)

    load = pltpu.make_async_copy(a22, big, in_sem)
    load.start()

    def row_slot(dl, dx, dk):
        return ((lo + dl) % 2) * 8 + ((x + dx) % 4) * 2 + (k + dk) % 2

    def col_slot(dz, dy):
        return chunk_of(p, (z + dz) % 4, (y + dy) % 4)

    def row_idx(dl, dx, dk, pc):
        return ((dl * 4 + dx) * 2 + dk) * 2 + pc

    def col_idx(dz, dy, pc):
        return (dz * 4 + dy) * 2 + pc

    started = []

    def send(src, dst, sem, peer):
        copy = pltpu.make_async_remote_copy(
            src_ref=src, dst_ref=dst, send_sem=send_sem.at[len(started)], recv_sem=sem,
            device_id=peer, device_id_type=MESH)
        copy.start()
        started.append(copy)

    def send_row(src, slot, pc, peer, dl, dx, dk):
        send(src, rows[pc].at[slot], row_sem.at[row_idx(dl, dx, dk, pc)], peer)

    def fwd_row(dl, dx, dk, pc, peer, there):
        slot = row_slot(dl, dx, dk)
        send_row(rows[pc].at[slot], slot, pc, peer, *there)

    def fwd_col(dz, dy, pc, peer, there):
        slot = col_slot(dz, dy)
        send(cols[pc].at[slot], cols[pc].at[slot], col_sem.at[col_idx(*there, pc)], peer)

    def got(ref, sem):
        pltpu.make_async_remote_copy(
            src_ref=ref, dst_ref=ref, send_sem=send_sem.at[0], recv_sem=sem,
            device_id=sib, device_id_type=MESH).wait_recv()

    def got_row(dl, dx, dk, pc):
        got(rows[pc].at[row_slot(dl, dx, dk)], row_sem.at[row_idx(dl, dx, dk, pc)])

    def got_col(dz, dy, pc):
        got(cols[pc].at[col_slot(dz, dy)], col_sem.at[col_idx(dz, dy, pc)])

    def to_sib(dl, dx, pc):
        fwd_row(dl, dx, 0, pc, sib, (dl, dx, 1))

    def col_out(dz):
        for pc in (A, L):
            fwd_col(dz, 0, pc, yu, (dz, 3))
            fwd_col(dz, 0, pc, yd, (dz, 1))

    def col_relay(dz):
        got_col(dz, 3, A)
        fwd_col(dz, 3, A, yu, (dz, 2))
        got_col(dz, 1, L)
        fwd_col(dz, 1, L, yd, (dz, 2))

    inv = linv[...]
    inv_t = inv.T
    diag = mult(mult(inv, a11[...]), inv_t)
    diag_o[...] = diag
    correction = 0.5 * mult(l21[...], diag)
    panel_o[...] = (mult(a21[...], inv_t) - correction) - correction
    for i, w in enumerate((inv, diag, inv_t)):
        hi, low = split(w)
        w_hi[:, 256 * i:256 * (i + 1)] = hi
        w_lo[:, 256 * i:256 * (i + 1)] = low
    row_a[p] = a21[...]
    row_l[p] = l21[...]

    pl.semaphore_wait(barrier, 10)

    for pc in (A, L):
        send(own[pc], cols[pc].at[p], col_sem.at[col_idx(0, 0, pc)], t_to)
    for pc in (A, L):
        send_row(own[pc], p, pc, par, 1, 0, 0)
        send_row(own[pc], p, pc, xu, 0, 3, 0)
        send_row(own[pc], p, pc, xd, 0, 1, 0)
        send_row(own[pc], p, pc, sib, 0, 0, 1)

    for pc in (A, L):
        got_row(1, 0, 0, pc)
        fwd_row(1, 0, 0, pc, xu, (1, 3, 0))
        fwd_row(1, 0, 0, pc, xd, (1, 1, 0))
        to_sib(1, 0, pc)
    got_row(0, 3, 0, A)
    fwd_row(0, 3, 0, A, xu, (0, 2, 0))
    got_row(0, 1, 0, L)
    fwd_row(0, 1, 0, L, xd, (0, 2, 0))
    got_row(0, 3, 0, L)
    got_row(0, 1, 0, A)
    for dx in (3, 1):
        for pc in (A, L):
            to_sib(0, dx, pc)

    for pc in (A, L):
        got_col(0, 0, pc)
        fwd_col(0, 0, pc, zu, (3, 0))
        fwd_col(0, 0, pc, zd, (1, 0))
        fwd_col(0, 0, pc, yu, (0, 3))
        fwd_col(0, 0, pc, yd, (0, 1))

    got_row(1, 3, 0, A)
    fwd_row(1, 3, 0, A, xu, (1, 2, 0))
    got_row(1, 1, 0, L)
    fwd_row(1, 1, 0, L, xd, (1, 2, 0))
    got_row(1, 3, 0, L)
    got_row(1, 1, 0, A)
    for dx in (3, 1):
        for pc in (A, L):
            to_sib(1, dx, pc)

    got_col(3, 0, A)
    fwd_col(3, 0, A, zu, (2, 0))
    got_col(1, 0, L)
    fwd_col(1, 0, L, zd, (2, 0))
    col_relay(0)
    got_col(3, 0, L)
    got_col(1, 0, A)
    col_out(3)
    col_out(1)

    for dl in (0, 1):
        for pc in (A, L):
            got_row(dl, 2, 0, pc)
            to_sib(dl, 2, pc)
    for dl in (0, 1):
        for dx in range(4):
            for pc in (A, L):
                got_row(dl, dx, 1, pc)

    @pl.loop(0, 16)
    def _(j):
        at = pl.ds(pl.multiple_of(j * 64, 64), 64)
        for pc in (A, L):
            hi, low = split(rows[pc][j])
            r_hi[at, 256 * pc:256 * (pc + 1)] = hi
            r_lo[at, 256 * pc:256 * (pc + 1)] = low

    for pc in (A, L):
        got_col(2, 0, pc)
    col_out(2)
    got_col(0, 3, L)
    got_col(0, 1, A)
    for pc in (A, L):
        got_col(0, 2, pc)
    col_relay(3)
    col_relay(1)
    load.wait()

    stores = []

    def update(pairs):
        l_c = jnp.concatenate([col_l[pl.ds(2 * i, 2)].reshape(128, 256) for i in pairs], axis=0)
        a_c = jnp.concatenate([col_a[pl.ds(2 * i, 2)].reshape(128, 256) for i in pairs], axis=0)
        l_hi, l_lo = split(l_c)
        a_hi, a_lo = split(a_c)
        both = nn(l_hi, w_hi[:, :512]) + nn(l_hi, w_lo[:, :512]) + nn(l_lo, w_hi[:, :512])
        right = nn(a_hi, w_hi[:, 512:]) + nn(a_hi, w_lo[:, 512:]) + nn(a_lo, w_hi[:, 512:])
        c = jnp.concatenate([both[:, :256], right - both[:, 256:]], axis=1)
        c_hi, c_lo = split(c)
        for m in range(4):
            at = slice(256 * m, 256 * (m + 1))
            u = nt(r_hi[at, :], c_hi) + nt(r_hi[at, :], c_lo) + nt(r_lo[at, :], c_hi)
            for n, i in enumerate(pairs):
                lanes = pl.ds(pl.multiple_of(i * 128, 128), 128)
                big[at, lanes] = big[at, lanes] - u[:, 128 * n:128 * (n + 1)]
        for i in pairs:
            lanes = pl.ds(pl.multiple_of(i * 128, 128), 128)
            copy = pltpu.make_async_copy(big.at[:, lanes], out.at[:, lanes], out_sem.at[len(stores)])
            copy.start()
            stores.append(copy)

    def pair(dz, dy):
        return col_slot(dz, dy) // 2

    for dz in (3, 1):
        got_col(dz, 3, L)
        got_col(dz, 1, A)
        for pc in (A, L):
            got_col(dz, 2, pc)
    update([pair(1, 0), pair(1, 1)])
    col_relay(2)
    update([pair(1, 2), pair(1, 3)])
    got_col(2, 3, L)
    got_col(2, 1, A)
    update([pair(0, 0), pair(0, 1)])
    for pc in (A, L):
        got_col(2, 2, pc)
    update([pair(0, 2), pair(0, 3)])

    for copy in started:
        copy.wait_send()
    for copy in stores:
        copy.wait()


def body(a11, linv11, a21, l21, a22):
    vmem = pl.BlockSpec(memory_space=pltpu.VMEM)
    anywhere = pl.BlockSpec(memory_space=pl.ANY)
    return pl.pallas_call(
        kernel,
        out_shape=(
            jax.ShapeDtypeStruct((256, 256), F32),
            jax.ShapeDtypeStruct((64, 256), F32),
            jax.ShapeDtypeStruct((1024, 1024), F32),
        ),
        in_specs=[vmem, vmem, vmem, vmem, anywhere],
        out_specs=(vmem, vmem, anywhere),
        scratch_shapes=[pltpu.VMEM((16, 64, 256), F32)] * 4
        + [pltpu.VMEM((1024, 512), BF16)] * 2
        + [pltpu.VMEM((256, 768), BF16)] * 2
        + [pltpu.VMEM((1024, 1024), F32)]
        + [
            pltpu.SemaphoreType.DMA((62,)),
            pltpu.SemaphoreType.DMA((32,)),
            pltpu.SemaphoreType.DMA((32,)),
            pltpu.SemaphoreType.DMA,
            pltpu.SemaphoreType.DMA((8,)),
        ],
        compiler_params=pltpu.CompilerParams(
            collective_id=0, has_side_effects=True, vmem_limit_bytes=40 * 2**20),
        name="panel_step",
    )(a11, linv11, a21, l21, a22)


def solution(mesh):
    panel_spec = P(("row", "col"), None)
    return jax.shard_map(
        body,
        mesh=mesh,
        in_specs=(P(), P(), panel_spec, panel_spec, P("row", "col")),
        out_specs=(P(), panel_spec, P("row", "col")),
        check_vma=False,
    )
```

time: 255 us -> 58.3 us (0.23)
  waiting for transfers between devices: 220 us -> 0 us
  Pallas kernels: 0 us -> 48.3 us
  matrix products: 14.6 us -> 0 us
  between operations: 14.1 us -> 0.65 us
  local copies, waits for them, and re-layouts: 2.58 us -> 9.1 us
    psum x1 -> x0, waiting for transfers between devices: 182 us -> none  [spread(): return lax.psum(kept, axis)]
    pallas_call x0 -> x1, Pallas kernels: none -> 48.3 us  [body(): pl.pallas_call(kernel, out_shape=(jax.ShapeDtypeStruct((256, 256), F32),...]
    all_gather x1 -> x0, waiting for transfers between devices: 38.5 us -> none  [body(): mine = lax.all_gather(packed, 'col', axis=0, tiled=True)]
    dot_general x5 -> x0, matrix products: 14.6 us -> none  [mult(): jnp.dot(a, b, precision=lax.Precision.HIGHEST, preferred_element_type=jnp...]
    unnamed x8 -> x13, local copies, waits for them, and re-layouts: 0.91 us -> 9.1 us
  transfers between devices with their start and end apart: 2 -> 0, of which waited for: 2 -> 0; matrix products, arithmetic and copies ran while one was open for 0% -> 0% of each run, Pallas kernels for 0% -> 0%
where the time goes in v1:
time: 58.3 us; the launch traced here: 58 us
  Pallas kernels  48.3 us (83%)
  local copies, waits for them, and re-layouts  9.1 us (16%)
  between operations  0.65 us (1%)
    pallas_call x1, Pallas kernels, body(): pl.pallas_call(kernel, out_shape=(jax.ShapeDtypeStruct((256, 256), F32),...  48.3 us
    unnamed x13, local copies, waits for them, and re-layouts  9.1 us

profile of v1, /device:TPU:6, one launch (start us, length us, event | category | flops | bytes accessed | tf_op | source)
XLA Modules:
  0.0 58.0 jit_solution(3874278402543964687)
XLA Ops:
  0.6 0.0 copy-start
  0.6 2.2 %copy-done = f32[1024,1024]{1,0:T(8,128)S(1)} copy-done((f32[1024,1024]{1,0:T(8,128)S(1)}, f32[1024,1024]{1,0:T(8,128)}, u32[]{:S(2)}) %copy-start) | copy-done | bytes 4194328
  2.8 0.0 copy-start.1
  2.8 0.9 %copy-done.1 = f32[256,256]{1,0:T(8,128)S(1)} copy-done((f32[256,256]{1,0:T(8,128)S(1)}, f32[256,256]{1,0:T(8,128)}, u32[]{:S(2)}) %copy-start.1) | copy-done | bytes 262168
  3.8 0.0 copy-start.2
  3.8 0.9 %copy-done.2 = f32[256,256]{1,0:T(8,128)S(1)} copy-done((f32[256,256]{1,0:T(8,128)S(1)}, f32[256,256]{1,0:T(8,128)}, u32[]{:S(2)}) %copy-start.2) | copy-done | bytes 262168
  4.7 0.0 copy-start.3
  4.7 0.8 %copy-done.3 = f32[64,256]{1,0:T(8,128)S(1)} copy-done((f32[64,256]{1,0:T(8,128)S(1)}, f32[64,256]{1,0:T(8,128)}, u32[]{:S(2)}) %copy-start.3) | copy-done | bytes 65560
  5.6 0.0 copy-start.4
  5.6 0.8 %copy-done.4 = f32[64,256]{1,0:T(8,128)S(1)} copy-done((f32[64,256]{1,0:T(8,128)S(1)}, f32[64,256]{1,0:T(8,128)}, u32[]{:S(2)}) %copy-start.4) | copy-done | bytes 65560
  6.4 48.3 %panel_step.1 = (f32[256,256]{1,0:T(8,128)S(1)}, f32[64,256]{1,0:T(8,128)S(1)}, f32[1024,1024]{1,0:T(8,128)S(1)}) custom-call(f32[256,256]{1,0:T(8,128)S(1)} %copy-done.1, f32[256,256]{1,0:T(8,128)S(1)} %copy-done.2, f32[64,256]{1,0:T(8,128)S(1)} %copy-done.3, f32[64,256]{1,0:T(8,128)S(1)} %copy-done.4, f32[1024,1024]{1,0:T(8,128)S(1)} %copy-done), custom_call_target="tpu_custom_call" | custom-call | tf_op jit(solution)/shard_map/panel_step/pallas_call | solution.py:274
  54.7 0.7 %copy.11 = f32[256,256]{1,0:T(8,128)} copy(f32[256,256]{1,0:T(8,128)S(1)} %get-tuple-element.6) | data formatting | bytes 524288
  55.4 0.6 %copy.12 = f32[64,256]{1,0:T(8,128)} copy(f32[64,256]{1,0:T(8,128)S(1)} %get-tuple-element.7) | data formatting | bytes 131072
  56.0 2.0 %copy.13 = f32[1024,1024]{1,0:T(8,128)} copy(f32[1024,1024]{1,0:T(8,128)S(1)} %get-tuple-element.8) | data formatting | bytes 8388608
Async XLA Ops:
  0.6 2.2 %copy-start = (f32[1024,1024]{1,0:T(8,128)S(1)}, f32[1024,1024]{1,0:T(8,128)}, u32[]{:S(2)}) copy-start(f32[1024,1024]{1,0:T(8,128)} %a22.1) | copy-start | bytes 12582916
  2.8 0.9 %copy-start.1 = (f32[256,256]{1,0:T(8,128)S(1)}, f32[256,256]{1,0:T(8,128)}, u32[]{:S(2)}) copy-start(f32[256,256]{1,0:T(8,128)} %a11.1) | copy-start | bytes 786436
  3.8 0.9 %copy-start.2 = (f32[256,256]{1,0:T(8,128)S(1)}, f32[256,256]{1,0:T(8,128)}, u32[]{:S(2)}) copy-start(f32[256,256]{1,0:T(8,128)} %linv.1) | copy-start | bytes 786436
  4.7 0.8 %copy-start.3 = (f32[64,256]{1,0:T(8,128)S(1)}, f32[64,256]{1,0:T(8,128)}, u32[]{:S(2)}) copy-start(f32[64,256]{1,0:T(8,128)} %a21.1) | copy-start | bytes 196612
  5.6 0.8 %copy-start.4 = (f32[64,256]{1,0:T(8,128)S(1)}, f32[64,256]{1,0:T(8,128)}, u32[]{:S(2)}) copy-start(f32[64,256]{1,0:T(8,128)} %l21.1) | copy-start | bytes 196612

commit v2 on v1

--- a/solution.py
+++ b/solution.py
@@ -43,8 +43,54 @@
     return ((zp + step) % 4) * 4 + (yp + 2 - xj + xp + 4) % 4
 
 
-def kernel(a11, linv, a21, l21, a22, diag_o, panel_o, out, row_a, row_l, col_a, col_l,
-           r_hi, r_lo, w_hi, w_lo, big, send_sem, row_sem, col_sem, in_sem, out_sem):
+def subtract(new, old, r_hi, r_lo, c_hi, c_lo, pairs, m):
+    at = slice(256 * m, 256 * (m + 1))
+    u = nt(r_hi[at, :], c_hi) + nt(r_hi[at, :], c_lo) + nt(r_lo[at, :], c_hi)
+    for n, i in enumerate(pairs):
+        lanes = pl.ds(pl.multiple_of(i * 128, 128), 128)
+        new[at, lanes] = old[at, lanes] - u[:, 128 * n:128 * (n + 1)]
+
+
+def last_pairs():
+    r, p = lax.axis_index("row"), lax.axis_index("col")
+    z, y = r // 4, r % 4
+    return [chunk_of(p, z, (y + dy) % 4) // 2 for dy in (2, 3)]
+
+
+def finish(big, diag, panel, r_hi, r_lo, c_hi, c_lo, diag_o, panel_o, out, done, sem):
+    r, p = lax.axis_index("row"), lax.axis_index("col")
+    z, y = r // 4, r % 4
+    copies = [
+        pltpu.make_async_copy(diag, diag_o, sem.at[0]),
+        pltpu.make_async_copy(panel, panel_o, sem.at[1]),
+    ]
+    for dz in (0, 1):
+        for dy in range(4):
+            if dz == 0 and dy >= 2:
+                continue
+            i = chunk_of(p, (z + dz) % 4, (y + dy) % 4) // 2
+            lanes = pl.ds(pl.multiple_of(i * 128, 128), 128)
+            copies.append(pltpu.make_async_copy(big.at[:, lanes], out.at[:, lanes], sem.at[len(copies)]))
+    for copy in copies:
+        copy.start()
+    pairs = last_pairs()
+    for m in range(4):
+        at = slice(256 * m, 256 * (m + 1))
+        u = nt(r_hi[at, :], c_hi[...]) + nt(r_hi[at, :], c_lo[...]) + nt(r_lo[at, :], c_hi[...])
+        for n, i in enumerate(pairs):
+            lanes = pl.ds(pl.multiple_of(i * 128, 128), 128)
+            done[at, 128 * n:128 * (n + 1)] = big[at, lanes] - u[:, 128 * n:128 * (n + 1)]
+            copy = pltpu.make_async_copy(
+                done.at[at, 128 * n:128 * (n + 1)], out.at[at, lanes], sem.at[len(copies)])
+            copy.start()
+            copies.append(copy)
+    for copy in copies:
+        copy.wait()
+
+
+def kernel(a11_h, linv_h, a21_h, l21_h, a22, diag_o, panel_o, big, r_hi, r_lo, c_hi, c_lo,
+           a11, linv, a21, l21, row_a, row_l, col_a, col_l, w_hi, w_lo,
+           send_sem, row_sem, col_sem, in_sem):
     r = lax.axis_index("row")
     p = lax.axis_index("col")
     z, y = r // 4, r % 4
@@ -68,8 +114,13 @@
     for peer in (sib, par, xu, xd, zu, zd, yu, yd, t_to, t_from):
         pl.semaphore_signal(barrier, inc=1, device_id=peer, device_id_type=MESH)
 
-    load = pltpu.make_async_copy(a22, big, in_sem)
-    load.start()
+    loads = [
+        pltpu.make_async_copy(src, dst, in_sem.at[i])
+        for i, (src, dst) in enumerate(
+            ((a21_h, a21), (l21_h, l21), (linv_h, linv), (a11_h, a11), (a22, big)))
+    ]
+    for copy in loads:
+        copy.start()
 
     def row_slot(dl, dx, dk):
         return ((lo + dl) % 2) * 8 + ((x + dx) % 4) * 2 + (k + dk) % 2
@@ -120,7 +171,7 @@
     def col_out(dz):
         for pc in (A, L):
             fwd_col(dz, 0, pc, yu, (dz, 3))
-            fwd_col(dz, 0, pc, yd, (dz, 1))
+            fwd_col(dz, 0, 1 - pc, yd, (dz, 1))
 
     def col_relay(dz):
         got_col(dz, 3, A)
@@ -128,6 +179,8 @@
         got_col(dz, 1, L)
         fwd_col(dz, 1, L, yd, (dz, 2))
 
+    for copy in loads[:4]:
+        copy.wait()
     inv = linv[...]
     inv_t = inv.T
     diag = mult(mult(inv, a11[...]), inv_t)
@@ -148,13 +201,14 @@
     for pc in (A, L):
         send_row(own[pc], p, pc, par, 1, 0, 0)
         send_row(own[pc], p, pc, xu, 0, 3, 0)
-        send_row(own[pc], p, pc, xd, 0, 1, 0)
+        send_row(own[1 - pc], p, 1 - pc, xd, 0, 1, 0)
         send_row(own[pc], p, pc, sib, 0, 0, 1)
 
     for pc in (A, L):
         got_row(1, 0, 0, pc)
+    for pc in (A, L):
         fwd_row(1, 0, 0, pc, xu, (1, 3, 0))
-        fwd_row(1, 0, 0, pc, xd, (1, 1, 0))
+        fwd_row(1, 0, 0, 1 - pc, xd, (1, 1, 0))
         to_sib(1, 0, pc)
     got_row(0, 3, 0, A)
     fwd_row(0, 3, 0, A, xu, (0, 2, 0))
@@ -166,12 +220,16 @@
         for pc in (A, L):
             to_sib(0, dx, pc)
 
-    for pc in (A, L):
-        got_col(0, 0, pc)
-        fwd_col(0, 0, pc, zu, (3, 0))
-        fwd_col(0, 0, pc, zd, (1, 0))
-        fwd_col(0, 0, pc, yu, (0, 3))
-        fwd_col(0, 0, pc, yd, (0, 1))
+    got_col(0, 0, A)
+    fwd_col(0, 0, A, zu, (3, 0))
+    fwd_col(0, 0, A, yu, (0, 3))
+    got_col(0, 0, L)
+    fwd_col(0, 0, L, zd, (1, 0))
+    fwd_col(0, 0, L, yd, (0, 1))
+    fwd_col(0, 0, L, zu, (3, 0))
+    fwd_col(0, 0, A, zd, (1, 0))
+    fwd_col(0, 0, L, yu, (0, 3))
+    fwd_col(0, 0, A, yd, (0, 1))
 
     got_row(1, 3, 0, A)
     fwd_row(1, 3, 0, A, xu, (1, 2, 0))
@@ -219,30 +277,21 @@
         got_col(0, 2, pc)
     col_relay(3)
     col_relay(1)
-    load.wait()
-
-    stores = []
-
-    def update(pairs):
+    loads[4].wait()
+
+    def operand(pairs):
         l_c = jnp.concatenate([col_l[pl.ds(2 * i, 2)].reshape(128, 256) for i in pairs], axis=0)
         a_c = jnp.concatenate([col_a[pl.ds(2 * i, 2)].reshape(128, 256) for i in pairs], axis=0)
         l_hi, l_lo = split(l_c)
         a_hi, a_lo = split(a_c)
         both = nn(l_hi, w_hi[:, :512]) + nn(l_hi, w_lo[:, :512]) + nn(l_lo, w_hi[:, :512])
         right = nn(a_hi, w_hi[:, 512:]) + nn(a_hi, w_lo[:, 512:]) + nn(a_lo, w_hi[:, 512:])
-        c = jnp.concatenate([both[:, :256], right - both[:, 256:]], axis=1)
-        c_hi, c_lo = split(c)
+        return split(jnp.concatenate([both[:, :256], right - both[:, 256:]], axis=1))
+
+    def update(pairs):
+        hi, low = operand(pairs)
         for m in range(4):
-            at = slice(256 * m, 256 * (m + 1))
-            u = nt(r_hi[at, :], c_hi) + nt(r_hi[at, :], c_lo) + nt(r_lo[at, :], c_hi)
-            for n, i in enumerate(pairs):
-                lanes = pl.ds(pl.multiple_of(i * 128, 128), 128)
-                big[at, lanes] = big[at, lanes] - u[:, 128 * n:128 * (n + 1)]
-        for i in pairs:
-            lanes = pl.ds(pl.multiple_of(i * 128, 128), 128)
-            copy = pltpu.make_async_copy(big.at[:, lanes], out.at[:, lanes], out_sem.at[len(stores)])
-            copy.start()
-            stores.append(copy)
+            subtract(big, big, r_hi, r_lo, hi, low, pairs, m)
 
     def pair(dz, dy):
         return col_slot(dz, dy) // 2
@@ -260,41 +309,50 @@
     update([pair(0, 0), pair(0, 1)])
     for pc in (A, L):
         got_col(2, 2, pc)
-    update([pair(0, 2), pair(0, 3)])
+    hi, low = operand(last_pairs())
+    c_hi[...] = hi
+    c_lo[...] = low
 
     for copy in started:
         copy.wait_send()
-    for copy in stores:
-        copy.wait()
 
 
 def body(a11, linv11, a21, l21, a22):
     vmem = pl.BlockSpec(memory_space=pltpu.VMEM)
-    anywhere = pl.BlockSpec(memory_space=pl.ANY)
-    return pl.pallas_call(
+    hbm = pl.BlockSpec(memory_space=pltpu.HBM)
+    shape = jax.ShapeDtypeStruct
+    square, tall, whole = shape((256, 256), F32), shape((64, 256), F32), shape((1024, 1024), F32)
+    diag, panel, big, r_hi, r_lo, c_hi, c_lo = pl.pallas_call(
         kernel,
-        out_shape=(
-            jax.ShapeDtypeStruct((256, 256), F32),
-            jax.ShapeDtypeStruct((64, 256), F32),
-            jax.ShapeDtypeStruct((1024, 1024), F32),
-        ),
-        in_specs=[vmem, vmem, vmem, vmem, anywhere],
-        out_specs=(vmem, vmem, anywhere),
-        scratch_shapes=[pltpu.VMEM((16, 64, 256), F32)] * 4
-        + [pltpu.VMEM((1024, 512), BF16)] * 2
+        out_shape=(square, tall, whole)
+        + (shape((1024, 512), BF16),) * 2
+        + (shape((256, 512), BF16),) * 2,
+        in_specs=[hbm] * 5,
+        out_specs=(vmem,) * 7,
+        scratch_shapes=[pltpu.VMEM((256, 256), F32)] * 2
+        + [pltpu.VMEM((64, 256), F32)] * 2
+        + [pltpu.VMEM((16, 64, 256), F32)] * 4
         + [pltpu.VMEM((256, 768), BF16)] * 2
-        + [pltpu.VMEM((1024, 1024), F32)]
         + [
             pltpu.SemaphoreType.DMA((62,)),
             pltpu.SemaphoreType.DMA((32,)),
             pltpu.SemaphoreType.DMA((32,)),
-            pltpu.SemaphoreType.DMA,
-            pltpu.SemaphoreType.DMA((8,)),
+            pltpu.SemaphoreType.DMA((5,)),
         ],
         compiler_params=pltpu.CompilerParams(
-            collective_id=0, has_side_effects=True, vmem_limit_bytes=40 * 2**20),
+            collective_id=0, has_side_effects=True, vmem_limit_bytes=30 * 2**20),
         name="panel_step",
-    )(a11, linv11, a21, l21, a22)
+    )(*(pltpu.with_memory_space_constraint(v, pltpu.HBM) for v in (a11, linv11, a21, l21, a22)))
+    diag, panel, trailing = pl.pallas_call(
+        finish,
+        out_shape=(square, tall, whole),
+        in_specs=[vmem] * 7,
+        out_specs=(hbm,) * 3,
+        scratch_shapes=[pltpu.VMEM((1024, 256), F32), pltpu.SemaphoreType.DMA((16,))],
+        compiler_params=pltpu.CompilerParams(vmem_limit_bytes=30 * 2**20),
+        name="last_columns",
+    )(big, diag, panel, r_hi, r_lo, c_hi, c_lo)
+    return diag, panel, trailing
 
 
 def solution(mesh):

time: 58.3 us -> 50.7 us (0.87)
  local copies, waits for them, and re-layouts: 9.1 us -> 0 us
  Pallas kernels: 48.3 us -> 49.9 us
    unnamed x13 -> x0, local copies, waits for them, and re-layouts: 9.1 us -> none
    pallas_call x1 -> x2, Pallas kernels: 48.3 us -> 49.9 us  [the longest x1 47.2 us: body(): pl.pallas_call(kernel, out_shape=(square, tall, whole) + (shape((1024, 51...]
where the time goes in v2:
time: 50.7 us; the launch traced here: 50.6 us
  Pallas kernels  49.9 us (98%)
  between operations  0.64 us (1%)
    pallas_call x1, Pallas kernels, body(): pl.pallas_call(kernel, out_shape=(square, tall, whole) + (shape((1024, 51...  47.2 us
    pallas_call x1, Pallas kernels, body(): pl.pallas_call(finish, out_shape=(square, tall, whole), in_specs=[vmem] *...  2.7 us

profile of v2, /device:TPU:6, one launch (start us, length us, event | category | flops | bytes accessed | tf_op | source)
XLA Modules:
  0.0 50.6 jit_solution(609773147369323100)
XLA Ops:
  0.6 47.2 %panel_step.1 = (f32[256,256]{1,0:T(8,128)S(1)}, f32[64,256]{1,0:T(8,128)S(1)}, f32[1024,1024]{1,0:T(8,128)S(1)}, bf16[1024,512]{1,0:T(8,128)(2,1)S(1)}, bf16[10...) custom-call(f32[256,256]{1,0:T(8,128)} %a11_h.1, f32[256,256]{1,0:T(8,128)} %linv_h.1, ...), custom_call_target="tpu_custom_call" | custom-call | tf_op jit(solution)/shard_map/panel_step/pallas_call | solution.py:325
  47.9 2.7 %last_columns.1 = (f32[256,256]{1,0:T(8,128)}, f32[64,256]{1,0:T(8,128)}, f32[1024,1024]{1,0:T(8,128)}) custom-call(f32[1024,1024]{1,0:T(8,128)S(1)} %get-tuple-element.10.big, f32[256,256]{1,0:T(8,128)S(1)} %get-tuple-element.11.diag, f32[64,256]{1,0:T(8,128)S(1)} %get-tuple-element.12.panel, bf16[1024,512]{1,0:T(8,128)(2,1)S(1)} %get-tuple-element.13.r_hi, ...), custom_call_target="tpu_custom_call" | custom-call | tf_op jit(solution)/shard_map/last_columns/pallas_call | solution.py:346
